TPU v7x, 512 devices: a whole 4x8x8 slice. The times are simulated.
512 devices in a mesh: scen: 8 (over x, core), bus: 64 (over y, z).
Axes of the slice: x: 4, y: 8, z: 8, core: 2. Of those that a mesh axis runs over, the one named last changes fastest.
Arguments:
- injections: bfloat16 [1024, 16384], P(('scen', 'bus')), may hold values from -6 to 6
- tile_values: bfloat16 [4096, 128, 128], P('bus', 'scen'), may hold values from -0.109375 to 0.109375
- tile_line: int32 [4096], P('bus'), may hold values from 0 to 191, as said below
- tile_bus: int32 [4096], P('bus'), may hold values from 0 to 1
- flow_pred: bfloat16 [1024, 24576], P('scen', 'bus'), may hold values from -6 to 6
- line_limit: int32 [24576], P('bus'), may hold values from 50 to 199
Outputs:
- grad_injections: bfloat16 [1024, 16384], P(('scen', 'bus'))
- flows: float32 [1024, 24576], P('scen', 'bus')
Inputs may be any that keep to these rules, and one draw needn't show every extreme that they name: `tile_line`: tile t is held by bus index t // 64; line block b is owned by bus index b // 3. Of the 64 tiles of one bus index at most 2 have line blocks of one owner, and in every draw some owner gets exactly 2 tiles from every bus index. A pair of line block and bus block may occur in several tiles; their values add.
All inputs are finite; a program needn't handle non-finite values.
Results may differ from a plain program's by a relative error of at most 0.0039.
Values may be sent and summed in bfloat16 or wider, within the bound.
No kernel may reach another device: no remote copies, remote signals or barrier semaphores. Data moves between devices by JAX's collectives and lax.ppermute only.
A program may use at most 64 MiB of HBM per device.

v0:
```python
import jax
import jax.numpy as jnp
from jax import lax
from jax.sharding import PartitionSpec as P


def per_device(injections, tile_values, tile_line, tile_bus, flow_pred, line_limit):
    bus_count = lax.axis_size("bus")
    local_inj = lax.all_to_all(injections, "bus", split_axis=1, concat_axis=0, tiled=True)
    tile_full = lax.all_gather(tile_values, "scen", axis=1, tiled=True)
    tile_count = tile_full.shape[0]
    tile_size = tile_full.shape[1]
    row_count = local_inj.shape[0]
    blocks_here = local_inj.shape[1] // tile_size
    line_blocks = flow_pred.shape[1] // tile_size
    per_owner = tile_count // bus_count
    capacity = per_owner + max(1, tile_count // (2 * bus_count))
    slot_total = bus_count * capacity
    inj_blocks = local_inj.reshape(row_count, blocks_here, tile_size)
    per_tile_inj = jnp.take(inj_blocks, tile_bus, axis=1)
    partial_flows = jnp.einsum(
        "stb,tlb->tsl", per_tile_inj, tile_full, preferred_element_type=jnp.float32
    )
    owner_index = tile_line // line_blocks
    within_owner = tile_line % line_blocks
    owner_hits = (owner_index[:, None] == jnp.arange(bus_count, dtype=jnp.int32)[None, :]).astype(
        jnp.int32
    )
    rank_within = jnp.sum(jnp.cumsum(owner_hits, axis=0) * owner_hits, axis=1) - 1
    slot_index = owner_index * capacity + rank_within
    send_buffer = (
        jnp.zeros((slot_total, row_count, tile_size), jnp.float32).at[slot_index].set(partial_flows)
    )
    slot_label = jnp.full((slot_total,), -1, jnp.int32).at[slot_index].set(within_owner)
    received, received_label = (
        lax.all_to_all(send_buffer, "bus", split_axis=0, concat_axis=0, tiled=True),
        lax.all_to_all(slot_label, "bus", split_axis=0, concat_axis=0, tiled=True),
    )
    select_mask = (
        received_label[None, :] == jnp.arange(line_blocks, dtype=jnp.int32)[:, None]
    ).astype(jnp.float32)
    flow_blocks = jnp.einsum("ms,srl->rml", select_mask, received, precision=lax.Precision.HIGHEST)
    flows = flow_blocks.reshape(row_count, line_blocks * tile_size)
    line_cap = line_limit.astype(jnp.float32) * 0.01
    residual = flows - flow_pred.astype(jnp.float32)
    grad_flow = (
        residual
        + jax.nn.sigmoid(4.0 * (flows - line_cap))
        - jax.nn.sigmoid(4.0 * (-flows - line_cap))
    ).astype(jnp.bfloat16)
    gathered = lax.all_gather(grad_flow, "bus", axis=1, tiled=True)
    gathered_blocks = gathered.reshape(row_count, gathered.shape[1] // tile_size, tile_size)
    per_tile_grad = jnp.take(gathered_blocks, tile_line, axis=1)
    contrib = jnp.einsum(
        "stl,tlb->stb", per_tile_grad, tile_full, preferred_element_type=jnp.float32
    )
    bus_select = (tile_bus[:, None] == jnp.arange(blocks_here, dtype=jnp.int32)[None, :]).astype(
        jnp.float32
    )
    grad_blocks_bus = jnp.einsum(
        "stb,tk->skb", contrib, bus_select, precision=lax.Precision.HIGHEST
    )
    grad_local = grad_blocks_bus.reshape(row_count, blocks_here * tile_size).astype(jnp.bfloat16)
    grad_injections = lax.all_to_all(grad_local, "bus", split_axis=0, concat_axis=1, tiled=True)
    return (grad_injections, flows)


def solution(mesh):
    return jax.shard_map(
        per_device,
        mesh=mesh,
        in_specs=(
            P(("scen", "bus"), None),
            P("bus", "scen", None),
            P("bus"),
            P("bus"),
            P("scen", "bus"),
            P("bus"),
        ),
        out_specs=(P(("scen", "bus"), None), P("scen", "bus")),
        check_vma=False,
    )
```

profile of v0, /device:TPU:2, one launch (start us, length us, event | category | flops | bytes accessed | tf_op | source)
XLA Modules:
  0.0 535.0 jit_solution(14193557377811817124)
XLA Ops:
  7.2 0.7 all-gather.3.cloned.1.call-update
  7.9 16.6 %all-to-all-start = ((bf16[2,64,256]{2,0,1:T(2,128)(2,1)}), bf16[2,64,256]{2,0,1:T(2,128)(2,1)S(1)}, u32[]{:S(2)}, u32[]{:S(2)}) async-start(bf16[2,64,256]{2,0,1:T(2,128)(2,1)} %bitcast.34), calls=%async_computation | async-start | bytes 131072 | tf_op jit(solution)/shard_map/all_to_all | solution.py:9
  26.9 0.8 scatter_custom_fusion.1
  27.6 0.8 all_to_all.37
  28.4 8.4 %all-to-all-done = bf16[2,64,256]{2,0,1:T(2,128)(2,1)S(1)} async-done(((bf16[2,64,256]{2,0,1:T(2,128)(2,1)}), bf16[2,64,256]{2,0,1:T(2,128)(2,1)S(1)}, u32[]{:S(2)}, u32[]{:S(2)}) %all-to-all-start) | async-done | bytes 65568 | tf_op jit(solution)/shard_map/all_to_all | solution.py:9
  36.8 4.6 all-to-all-start.2
  41.4 1.0 gather_fusion
  42.4 4.4 all-gather.3.cloned.1.call-done
  46.9 5.2 fusion.5
  52.0 4.3 broadcast_in_dim.41
  56.3 12.0 %scatter_fusion = f32[128,128,128]{2,1,0:T(8,128)} fusion(f32[128,128,128]{2,1,0:T(8,128)} %broadcast_in_dim.41, s32[64]{0:T(128)S(1)} %compare_select_fusion.1, f32[64,128,128]{2,1,0:T(8,128)} %fusion.5), kind=kCustom, calls=%fused_computation.2 | custom fusion | bytes 12583168 | tf_op jit(solution)/shard_map/scatter | solution.py:32
  68.4 13.8 %all-to-all-start.1 = ((f32[128,128,128]{2,1,0:T(8,128)}), f32[128,128,128]{2,1,0:T(8,128)}, u32[]{:S(2)}, u32[]{:S(2)}) async-start(f32[128,128,128]{2,1,0:T(8,128)} %scatter_fusion), calls=%async_computation.1 | async-start | bytes 16777216 | tf_op jit(solution)/shard_map/all_to_all | solution.py:36
  83.0 0.7 reduce.3
  83.9 234.9 %all-to-all-done.1 = f32[128,128,128]{2,1,0:T(8,128)} async-done(((f32[128,128,128]{2,1,0:T(8,128)}), f32[128,128,128]{2,1,0:T(8,128)}, u32[]{:S(2)}, u32[]{:S(2)}) %all-to-all-start.1) | async-done | bytes 8388640 | tf_op jit(solution)/shard_map/all_to_all | solution.py:36
  318.8 10.4 %fusion.11 = f32[128,3,128]{2,1,0:T(4,128)S(1)} fusion(f32[128,128,128]{2,1,0:T(8,128)} %all-to-all-done.1, s32[128]{0:T(128)S(1)} %eq.49), kind=kOutput, calls=%fused_computation.16 | convolution fusion | flops 75497856 | bytes 8585728 | tf_op jit(solution)/shard_map/ms,srl->rml/dot_general | solution.py:42
  329.4 0.8 subtract_convert_fusion
  330.3 157.1 %all-gather.5.cloned.1.call-done = bf16[128,24576]{0,1:T(8,128)(2,1)} async-done(((bf16[128,384]{0,1:T(8,128)(2,1)}), bf16[128,24576]{0,1:T(8,128)(2,1)}) %all-gather.5.cloned.1.call-update) | async-done | bytes 6291472 | tf_op jit(solution)/shard_map/all_gather | solution.py:51
  487.4 8.7 %copy.31 = bf16[128,192,128]{2,0,1:T(8,128)(2,1)} copy(bf16[128,192,128]{0,2,1:T(8,128)(2,1)} %bitcast.30) | data formatting | bytes 12582912 | tf_op jit(solution)/shard_map/reshape | solution.py:52
  496.0 3.7 gather_fusion.1
  499.8 2.4 convolution_bitcast_fusion
  502.1 3.8 fusion.17
  506.6 8.6 %all-to-all-start.3 = ((bf16[64,2,256]{2,1,0:T(2,128)(2,1)}), bf16[64,2,256]{2,1,0:T(2,128)(2,1)S(1)}, u32[]{:S(2)}, u32[]{:S(2)}) async-start(bf16[64,2,256]{2,1,0:T(2,128)(2,1)} %convert_element_type.30), calls=%async_computation.3 | async-start | bytes 131072 | tf_op jit(solution)/shard_map/all_to_all | solution.py:64
  515.2 0.8 copy.34
  516.0 11.5 %all-to-all-done.3 = bf16[64,2,256]{2,1,0:T(2,128)(2,1)S(1)} async-done(((bf16[64,2,256]{2,1,0:T(2,128)(2,1)}), bf16[64,2,256]{2,1,0:T(2,128)(2,1)S(1)}, u32[]{:S(2)}, u32[]{:S(2)}) %all-to-all-start.3) | async-done | bytes 65568 | tf_op jit(solution)/shard_map/all_to_all | solution.py:64
  (31 shorter events, 4.9 us)
Async XLA Ops:
  7.2 39.7 %all-gather.3.cloned.1.call-start = ((), (), s32[]{:S(2)}) async-start(), calls=%async_computation.4 | async-start | bytes 2359296 | tf_op jit(solution)/shard_map/all_gather | solution.py:10
  7.9 28.9 %all-to-all-start = ((bf16[2,64,256]{2,0,1:T(2,128)(2,1)}), bf16[2,64,256]{2,0,1:T(2,128)(2,1)S(1)}, u32[]{:S(2)}, u32[]{:S(2)}) async-start(bf16[2,64,256]{2,0,1:T(2,128)(2,1)} %bitcast.34), calls=%async_computation | async-start | bytes 131072 | tf_op jit(solution)/shard_map/all_to_all | solution.py:9
  36.8 31.6 %all-to-all-start.2 = ((s32[64,2,1]{1,2,0:T(1,128)}), s32[64,2,1]{1,2,0:T(1,128)S(1)}, u32[]{:S(2)}, u32[]{:S(2)}) async-start(s32[64,2,1]{1,2,0:T(1,128)} %bitcast.4), calls=%async_computation.2 | async-start | bytes 65536 | tf_op jit(solution)/shard_map/all_to_all | solution.py:37
  68.3 14.0 %copy-start = (bf16[128,384]{1,0:T(8,128)(2,1)S(1)}, bf16[128,384]{1,0:T(8,128)(2,1)}, u32[]{:S(2)}) copy-start(bf16[128,384]{1,0:T(8,128)(2,1)} %param.10) | copy-start | bytes 294916
  68.3 14.1 %copy-start.1 = (s32[384]{0:T(512)S(1)}, s32[384]{0:T(512)}, u32[]{:S(2)}) copy-start(s32[384]{0:T(512)} %param.11) | copy-start | bytes 4612
  68.4 250.5 %all-to-all-start.1 = ((f32[128,128,128]{2,1,0:T(8,128)}), f32[128,128,128]{2,1,0:T(8,128)}, u32[]{:S(2)}, u32[]{:S(2)}) async-start(f32[128,128,128]{2,1,0:T(8,128)} %scatter_fusion), calls=%async_computation.1 | async-start | bytes 16777216 | tf_op jit(solution)/shard_map/all_to_all | solution.py:36
  82.1 405.2 %all-gather.5.cloned.1.call-start = ((), (), s32[]{:S(2)}) async-start(), calls=%async_computation.5 | async-start | bytes 6389760 | tf_op jit(solution)/shard_map/all_gather | solution.py:51
  83.9 246.4 %copy-start.3 = (s32[64]{0:T(128)S(1)}, s32[64]{0:T(128)}, u32[]{:S(2)}) copy-start(s32[64]{0:T(128)} %param.8) | copy-start | bytes 772
  499.8 2.4 copy-start.2
  506.6 20.9 %all-to-all-start.3 = ((bf16[64,2,256]{2,1,0:T(2,128)(2,1)}), bf16[64,2,256]{2,1,0:T(2,128)(2,1)S(1)}, u32[]{:S(2)}, u32[]{:S(2)}) async-start(bf16[64,2,256]{2,1,0:T(2,128)(2,1)} %convert_element_type.30), calls=%async_computation.3 | async-start | bytes 131072 | tf_op jit(solution)/shard_map/all_to_all | solution.py:64
Sparse Core Ops, SparseCore 0:
  10.1 36.6 all-gather.2
  330.4 156.9 all-gather.4
where the time goes:
time: 536 us; the launch traced here: 535 us
  waiting for transfers between devices  417 us (78%)
  starting transfers between devices  43.8 us (8%)
  local copies, waits for them, and re-layouts  34.3 us (6%)
  matrix products  21.8 us (4%)
  between operations  14.2 us (3%)
    all_to_all x1, waiting for transfers between devices, per_device(): lax.all_to_all(send_buffer, 'bus', split_axis=0, concat_axis=0, tiled=True)  235 us
    all_gather x1, waiting for transfers between devices, per_device(): gathered = lax.all_gather(grad_flow, 'bus', axis=1, tiled=True)  157 us
    all_to_all x1, starting transfers between devices, per_device(): lax.all_to_all(injections, 'bus', split_axis=1, concat_axis=0, tiled=True)  16.6 us
    all_to_all x1, starting transfers between devices, per_device(): lax.all_to_all(send_buffer, 'bus', split_axis=0, concat_axis=0, tiled=True)  13.8 us
    scatter x1, local copies, waits for them, and re-layouts, per_device(): jnp.zeros((slot_total, row_count, tile_size), jnp.float32).at[slot_index]  12 us
    all_to_all x1, waiting for transfers between devices, per_device(): lax.all_to_all(grad_local, 'bus', split_axis=0, concat_axis=1, tiled=True)  11.5 us
  transfers between devices with their start and end apart: 6, of which 5 were waited for; matrix products, arithmetic and copies ran while one was open for 5% of the time, Pallas kernels for 0%

commit v1 on v0

--- a/solution.py
+++ b/solution.py
@@ -48,7 +48,10 @@
         + jax.nn.sigmoid(4.0 * (flows - line_cap))
         - jax.nn.sigmoid(4.0 * (-flows - line_cap))
     ).astype(jnp.bfloat16)
-    gathered = lax.all_gather(grad_flow, "bus", axis=1, tiled=True)
+    amount_of = lax.axis_size("bus")
+    items = [amount_of if num == 1 else 1 for num in range(grad_flow.ndim)]
+    field_out = jnp.tile(grad_flow, items)
+    gathered = lax.all_to_all(field_out, "bus", split_axis=1, concat_axis=1, tiled=True)
     gathered_blocks = gathered.reshape(row_count, gathered.shape[1] // tile_size, tile_size)
     per_tile_grad = jnp.take(gathered_blocks, tile_line, axis=1)
     contrib = jnp.einsum(

time: 536 us -> 658 us (1.23)
  the two profiles are of different devices: /device:TPU:2 before, /device:TPU:8 now
where the time goes in v1:
time: 658 us; the launch traced here: 657 us
  waiting for transfers between devices  462 us (70%)
  starting transfers between devices  117 us (18%)
  local copies, waits for them, and re-layouts  38.3 us (6%)
  matrix products  21.7 us (3%)
  between operations  14.2 us (2%)
    all_to_all x1, waiting for transfers between devices, per_device(): lax.all_to_all(send_buffer, 'bus', split_axis=0, concat_axis=0, tiled=True)  250 us
    all_to_all x1, waiting for transfers between devices, per_device(): lax.all_to_all(field_out, 'bus', split_axis=1, concat_axis=1, tiled=True)  188 us
    all_to_all x1, starting transfers between devices, per_device(): lax.all_to_all(field_out, 'bus', split_axis=1, concat_axis=1, tiled=True)  49.9 us
    all_to_all x1, starting transfers between devices, per_device(): lax.all_to_all(grad_local, 'bus', split_axis=0, concat_axis=1, tiled=True)  31.7 us
    all_to_all x1, starting transfers between devices, per_device(): lax.all_to_all(injections, 'bus', split_axis=1, concat_axis=0, tiled=True)  16.6 us
    all_to_all x1, starting transfers between devices, per_device(): lax.all_to_all(send_buffer, 'bus', split_axis=0, concat_axis=0, tiled=True)  13.8 us
  transfers between devices with their start and end apart: 6, of which 5 were waited for; matrix products, arithmetic and copies ran while one was open for 4% of the time, Pallas kernels for 0%

profile of v1, /device:TPU:8, one launch (start us, length us, event | category | flops | bytes accessed | tf_op | source)
XLA Modules:
  0.0 656.7 jit_solution(9815568015619625779)
XLA Ops:
  7.9 16.6 %all-to-all-start = ((bf16[2,64,256]{2,0,1:T(2,128)(2,1)}), bf16[2,64,256]{2,0,1:T(2,128)(2,1)S(1)}, u32[]{:S(2)}, u32[]{:S(2)}) async-start(bf16[2,64,256]{2,0,1:T(2,128)(2,1)} %bitcast.33), calls=%async_computation | async-start | bytes 131072 | tf_op jit(solution)/shard_map/all_to_all | solution.py:9
  26.9 0.8 scatter_custom_fusion.1
  27.6 0.8 all_to_all.41
  28.4 7.5 %all-to-all-done = bf16[2,64,256]{2,0,1:T(2,128)(2,1)S(1)} async-done(((bf16[2,64,256]{2,0,1:T(2,128)(2,1)}), bf16[2,64,256]{2,0,1:T(2,128)(2,1)S(1)}, u32[]{:S(2)}, u32[]{:S(2)}) %all-to-all-start) | async-done | bytes 65568 | tf_op jit(solution)/shard_map/all_to_all | solution.py:9
  35.9 5.4 all-to-all-start.2
  41.4 1.0 gather_fusion
  42.3 4.9 all-gather.2.cloned.1.call-done
  47.2 5.2 fusion.5
  52.4 4.3 broadcast_in_dim.41
  56.7 11.9 %scatter_fusion = f32[128,128,128]{2,1,0:T(8,128)} fusion(f32[128,128,128]{2,1,0:T(8,128)} %broadcast_in_dim.41, s32[64]{0:T(128)S(1)} %compare_select_fusion.1, f32[64,128,128]{2,1,0:T(8,128)} %fusion.5), kind=kCustom, calls=%fused_computation.2 | custom fusion | bytes 12583168 | tf_op jit(solution)/shard_map/scatter | solution.py:32
  68.6 13.8 %all-to-all-start.1 = ((f32[128,128,128]{2,1,0:T(8,128)}), f32[128,128,128]{2,1,0:T(8,128)}, u32[]{:S(2)}, u32[]{:S(2)}) async-start(f32[128,128,128]{2,1,0:T(8,128)} %scatter_fusion), calls=%async_computation.1 | async-start | bytes 16777216 | tf_op jit(solution)/shard_map/all_to_all | solution.py:36
  83.1 0.7 reduce.3
  84.0 250.0 %all-to-all-done.1 = f32[128,128,128]{2,1,0:T(8,128)} async-done(((f32[128,128,128]{2,1,0:T(8,128)}), f32[128,128,128]{2,1,0:T(8,128)}, u32[]{:S(2)}, u32[]{:S(2)}) %all-to-all-start.1) | async-done | bytes 8388640 | tf_op jit(solution)/shard_map/all_to_all | solution.py:36
  334.0 10.4 %fusion.11 = f32[128,3,128]{2,1,0:T(4,128)S(1)} fusion(f32[128,128,128]{2,1,0:T(8,128)} %all-to-all-done.1, s32[128]{0:T(128)S(1)} %eq.49), kind=kOutput, calls=%fused_computation.16 | convolution fusion | flops 75497856 | bytes 8585728 | tf_op jit(solution)/shard_map/ms,srl->rml/dot_general | solution.py:42
  344.8 4.2 tile.2
  349.0 49.9 %all-to-all-start.3 = ((bf16[128,64,384]{0,2,1:T(8,128)(2,1)}), bf16[128,64,384]{0,2,1:T(8,128)(2,1)}, u32[]{:S(2)}, u32[]{:S(2)}) async-start(bf16[128,64,384]{0,2,1:T(8,128)(2,1)} %tile.2), calls=%async_computation.3 | async-start | bytes 12582912 | tf_op jit(solution)/shard_map/all_to_all | solution.py:54
  398.9 188.0 %all-to-all-done.3 = bf16[128,64,384]{0,2,1:T(8,128)(2,1)} async-done(((bf16[128,64,384]{0,2,1:T(8,128)(2,1)}), bf16[128,64,384]{0,2,1:T(8,128)(2,1)}, u32[]{:S(2)}, u32[]{:S(2)}) %all-to-all-start.3) | async-done | bytes 6291488 | tf_op jit(solution)/shard_map/all_to_all | solution.py:54
  586.8 8.6 %copy.32 = bf16[128,192,128]{2,0,1:T(8,128)(2,1)} copy(bf16[128,192,128]{0,2,1:T(8,128)(2,1)} %bitcast.8) | data formatting | bytes 12582912 | tf_op jit(solution)/shard_map/reshape | solution.py:55
  595.4 3.7 gather_fusion.1
  599.2 2.4 convolution_bitcast_fusion
  601.6 3.8 fusion.17
  606.1 31.7 %all-to-all-start.4 = ((bf16[64,2,256]{2,1,0:T(2,128)(2,1)}), bf16[64,2,256]{2,1,0:T(2,128)(2,1)S(1)}, u32[]{:S(2)}, u32[]{:S(2)}) async-start(bf16[64,2,256]{2,1,0:T(2,128)(2,1)} %convert_element_type.30), calls=%async_computation.4 | async-start | bytes 131072 | tf_op jit(solution)/shard_map/all_to_all | solution.py:67
  637.8 0.8 copy.35
  638.6 10.6 %all-to-all-done.4 = bf16[64,2,256]{2,1,0:T(2,128)(2,1)S(1)} async-done(((bf16[64,2,256]{2,1,0:T(2,128)(2,1)}), bf16[64,2,256]{2,1,0:T(2,128)(2,1)S(1)}, u32[]{:S(2)}, u32[]{:S(2)}) %all-to-all-start.4) | async-done | bytes 65568 | tf_op jit(solution)/shard_map/all_to_all | solution.py:67
  (31 shorter events, 5.6 us)
Async XLA Ops:
  7.2 40.1 %all-gather.2.cloned.1.call-start = ((), (), s32[]{:S(2)}) async-start(), calls=%async_computation.5 | async-start | bytes 2359296 | tf_op jit(solution)/shard_map/all_gather | solution.py:10
  7.9 28.0 %all-to-all-start = ((bf16[2,64,256]{2,0,1:T(2,128)(2,1)}), bf16[2,64,256]{2,0,1:T(2,128)(2,1)S(1)}, u32[]{:S(2)}, u32[]{:S(2)}) async-start(bf16[2,64,256]{2,0,1:T(2,128)(2,1)} %bitcast.33), calls=%async_computation | async-start | bytes 131072 | tf_op jit(solution)/shard_map/all_to_all | solution.py:9
  35.9 32.7 %all-to-all-start.2 = ((s32[64,2,1]{1,2,0:T(1,128)}), s32[64,2,1]{1,2,0:T(1,128)S(1)}, u32[]{:S(2)}, u32[]{:S(2)}) async-start(s32[64,2,1]{1,2,0:T(1,128)} %bitcast.4), calls=%async_computation.2 | async-start | bytes 65536 | tf_op jit(solution)/shard_map/all_to_all | solution.py:37
  68.6 13.8 %copy-start = (bf16[128,384]{1,0:T(8,128)(2,1)S(1)}, bf16[128,384]{1,0:T(8,128)(2,1)}, u32[]{:S(2)}) copy-start(bf16[128,384]{1,0:T(8,128)(2,1)} %param.10) | copy-start | bytes 294916
  68.6 14.0 %copy-start.1 = (s32[384]{0:T(512)S(1)}, s32[384]{0:T(512)}, u32[]{:S(2)}) copy-start(s32[384]{0:T(512)} %param.11) | copy-start | bytes 4612
  68.6 265.4 %all-to-all-start.1 = ((f32[128,128,128]{2,1,0:T(8,128)}), f32[128,128,128]{2,1,0:T(8,128)}, u32[]{:S(2)}, u32[]{:S(2)}) async-start(f32[128,128,128]{2,1,0:T(8,128)} %scatter_fusion), calls=%async_computation.1 | async-start | bytes 16777216 | tf_op jit(solution)/shard_map/all_to_all | solution.py:36
  349.0 49.9 %copy-start.3 = (s32[64]{0:T(128)S(1)}, s32[64]{0:T(128)}, u32[]{:S(2)}) copy-start(s32[64]{0:T(128)} %param.8) | copy-start | bytes 772
  349.0 237.9 %all-to-all-start.3 = ((bf16[128,64,384]{0,2,1:T(8,128)(2,1)}), bf16[128,64,384]{0,2,1:T(8,128)(2,1)}, u32[]{:S(2)}, u32[]{:S(2)}) async-start(bf16[128,64,384]{0,2,1:T(8,128)(2,1)} %tile.2), calls=%async_computation.3 | async-start | bytes 12582912 | tf_op jit(solution)/shard_map/all_to_all | solution.py:54
  599.2 2.4 copy-start.2
  606.1 43.1 %all-to-all-start.4 = ((bf16[64,2,256]{2,1,0:T(2,128)(2,1)}), bf16[64,2,256]{2,1,0:T(2,128)(2,1)S(1)}, u32[]{:S(2)}, u32[]{:S(2)}) async-start(bf16[64,2,256]{2,1,0:T(2,128)(2,1)} %convert_element_type.30), calls=%async_computation.4 | async-start | bytes 131072 | tf_op jit(solution)/shard_map/all_to_all | solution.py:67
Sparse Core Ops, SparseCore 0:
  10.1 37.0 all-gather.1
